TPU v7x, 512 devices: a whole 4x4x16 slice. The times are simulated.
512 devices in a mesh: dp: 32 (over y, x, core), tensor: 16 (over z).
Axes of the slice: x: 4, y: 4, z: 16, core: 2. Of those that a mesh axis runs over, the one named last changes fastest.
Arguments:
- tokens: bfloat16 [14336, 8192], P('dp', 'tensor'), may hold values from -6 to 6
- weight: bfloat16 [8192, 2048], P('tensor'), may hold values from -0.09375 to 0.09375
- cotangent: bfloat16 [14336, 2048], P('dp', 'tensor'), may hold values from -6 to 6
- slot_job: int32 [448], replicated, may hold values from 0 to 447, as said below
- slot_count: int32 [448], P('dp'), may hold values from 1 to 32
- adapter_down: float32 [448, 8, 8192], P('dp', None, 'tensor'), may hold values from -0.0625 to 0.0625
- adapter_up: float32 [448, 8, 2048], P('dp', None, 'tensor'), may hold values from -1 to 1
- down_first: float32 [448, 8, 8192], P('dp', None, 'tensor'), may hold values from -4 to 4
- down_second: float32 [448, 8, 8192], P('dp', None, 'tensor'), may hold values from 0.01 to 1
- up_first: float32 [448, 8, 2048], P('dp', None, 'tensor'), may hold values from -4 to 4
- up_second: float32 [448, 8, 2048], P('dp', None, 'tensor'), may hold values from 0.01 to 1
Outputs:
- values: bfloat16 [14336, 2048], P('dp', 'tensor')
- token_grad: bfloat16 [14336, 8192], P('dp', 'tensor')
- new_down: float32 [448, 8, 8192], P('dp', None, 'tensor')
- new_down_first: float32 [448, 8, 8192], P('dp', None, 'tensor')
- new_down_second: float32 [448, 8, 8192], P('dp', None, 'tensor')
- new_up: float32 [448, 8, 2048], P('dp', None, 'tensor')
- new_up_first: float32 [448, 8, 2048], P('dp', None, 'tensor')
- new_up_second: float32 [448, 8, 2048], P('dp', None, 'tensor')
Inputs may be any that keep to these rules, and one draw needn't show every extreme that they name: `slot_job`: every job stands in exactly one slot. Slots 14 * g to 14 * g + 13 form token group g. The adapters and moments of job j are stored at dp index j // 14, and no group holds two jobs whose adapters are stored at the same dp index.
All inputs are finite; a program needn't handle non-finite values.
Results may differ from a plain program's by a relative error of at most 0.0028.
Values may be sent and summed in bfloat16 or wider, within the bound.
A program may use at most 64 MiB of HBM per device.

v0:
```python
import jax
import jax.numpy as jnp
from jax import lax
from jax.sharding import PartitionSpec as P

lowrank_scale = 2.0
learn_rate = 0.001
beta_first = 0.9
beta_second = 0.999
adam_eps = 1e-08
adam_step = 20.0


def adam_update(param, first, second, grad):
    new_first = beta_first * first + (1.0 - beta_first) * grad
    new_second = beta_second * second + (1.0 - beta_second) * grad * grad
    fix_first = 1.0 - beta_first**adam_step
    fix_second = 1.0 - beta_second**adam_step
    new_param = param - learn_rate * (new_first / fix_first) / (
        jnp.sqrt(new_second / fix_second) + adam_eps
    )
    return (new_param, new_first, new_second)


def per_device(
    tokens,
    weight,
    cotangent,
    slot_job,
    slot_count,
    adapter_down,
    adapter_up,
    down_first,
    down_second,
    up_first,
    up_second,
):
    highest = lax.Precision.HIGHEST
    slot_total = slot_count.shape[0]
    group_count = lax.axis_size("dp")
    group_id = lax.axis_index("dp")
    block_len = tokens.shape[0] // slot_total
    rank_len = adapter_down.shape[1]
    my_jobs = lax.dynamic_slice_in_dim(slot_job, group_id * slot_total, slot_total)
    group_ids = jnp.arange(group_count, dtype=jnp.int32)
    owner_hot = (my_jobs // slot_total)[:, None] == group_ids[None, :]
    owned_jobs = group_id * slot_total + jnp.arange(slot_total, dtype=jnp.int32)
    job_match = slot_job[None, :] == owned_jobs[:, None]
    all_slots = jnp.arange(slot_job.shape[0], dtype=jnp.int32)
    job_place = jnp.sum(jnp.where(job_match, all_slots[None, :], 0), axis=1)
    dest_hot = (job_place // slot_total)[:, None] == group_ids[None, :]
    down_half = adapter_down.astype(jnp.bfloat16)
    up_half = adapter_up.astype(jnp.bfloat16)
    pieces = (
        lax.all_gather(down_half, "dp", axis=0, tiled=True),
        lax.all_gather(up_half, "dp", axis=0, tiled=True),
    )
    piece_rows = pieces[0].shape[0]
    chosen = (my_jobs[:, None] == jnp.arange(piece_rows, dtype=jnp.int32)[None, :]).astype(
        jnp.bfloat16
    )
    down_sum = jnp.einsum("sc,crd->srd", chosen, pieces[0], preferred_element_type=jnp.float32)
    up_sum = jnp.einsum("sc,crk->srk", chosen, pieces[1], preferred_element_type=jnp.float32)
    down_slot = down_sum.astype(jnp.bfloat16)
    up_slot = up_sum.astype(jnp.bfloat16)
    tok_blocks = tokens.reshape(slot_total, block_len, tokens.shape[1])
    live_mask = (jnp.arange(block_len, dtype=jnp.int32)[None, :] < slot_count[:, None]).astype(
        jnp.bfloat16
    )
    masked_cot = (
        cotangent.reshape(slot_total, block_len, cotangent.shape[1]) * live_mask[:, :, None]
    )
    low_part = jnp.einsum(
        "bpd,brd->bpr", tok_blocks, down_slot, preferred_element_type=jnp.float32
    ).reshape(slot_total, block_len * rank_len)
    up_part = jnp.einsum(
        "bpk,brk->bpr", masked_cot, up_slot, preferred_element_type=jnp.float32
    ).reshape(slot_total, block_len * rank_len)
    low_flat, up_flat = lax.psum((low_part, up_part), "tensor")
    low_rank = low_flat.reshape(slot_total, block_len, rank_len)
    up_rank = up_flat.reshape(slot_total, block_len, rank_len)
    base_turned = lax.psum_scatter(
        lax.dot_general(
            weight, tokens, (((0,), (1,)), ((), ())), preferred_element_type=jnp.float32
        ),
        "tensor",
        scatter_dimension=0,
        tiled=True,
    )
    up_float = up_slot.astype(jnp.float32)
    down_float = down_slot.astype(jnp.float32)
    branch = jnp.einsum("bpr,brk->bpk", low_rank, up_float, precision=highest).reshape(
        tokens.shape[0], up_slot.shape[2]
    )
    values = (base_turned.T + lowrank_scale * branch).astype(jnp.bfloat16)
    cot_flat = masked_cot.reshape(tokens.shape[0], cotangent.shape[1])
    back_base = lax.dot_general(
        lax.all_gather(cot_flat, "tensor", axis=1, tiled=True),
        weight,
        (((1,), (1,)), ((), ())),
        preferred_element_type=jnp.float32,
    )
    back_branch = jnp.einsum("bpr,brd->bpd", up_rank, down_float, precision=highest).reshape(
        tokens.shape
    )
    token_grad = (back_base + lowrank_scale * back_branch).astype(jnp.bfloat16)
    factor = lowrank_scale / slot_count.astype(jnp.float32)
    grad_down_slot = factor[:, None, None] * jnp.einsum(
        "bpr,bpd->brd", up_rank, tok_blocks.astype(jnp.float32), precision=highest
    )
    grad_up_slot = factor[:, None, None] * jnp.einsum(
        "bpr,bpk->brk", low_rank, masked_cot.astype(jnp.float32), precision=highest
    )
    owner_float = owner_hot.astype(jnp.float32)
    send_grad_down = jnp.einsum("sg,srd->grd", owner_float, grad_down_slot, precision=highest)
    send_grad_up = jnp.einsum("sg,srk->grk", owner_float, grad_up_slot, precision=highest)
    back_down, back_up = (
        lax.all_to_all(send_grad_down, "dp", split_axis=0, concat_axis=0, tiled=True),
        lax.all_to_all(send_grad_up, "dp", split_axis=0, concat_axis=0, tiled=True),
    )
    dest_float = dest_hot.astype(jnp.float32)
    grad_down = jnp.einsum("sg,grd->srd", dest_float, back_down, precision=highest)
    grad_up = jnp.einsum("sg,grk->srk", dest_float, back_up, precision=highest)
    new_down, new_down_first, new_down_second = adam_update(
        adapter_down, down_first, down_second, grad_down
    )
    new_up, new_up_first, new_up_second = adam_update(adapter_up, up_first, up_second, grad_up)
    return (
        values,
        token_grad,
        new_down,
        new_down_first,
        new_down_second,
        new_up,
        new_up_first,
        new_up_second,
    )


def solution(mesh):
    in_specs = (
        P("dp", "tensor"),
        P("tensor", None),
        P("dp", "tensor"),
        P(),
        P("dp"),
        P("dp", None, "tensor"),
        P("dp", None, "tensor"),
        P("dp", None, "tensor"),
        P("dp", None, "tensor"),
        P("dp", None, "tensor"),
        P("dp", None, "tensor"),
    )
    out_specs = (
        P("dp", "tensor"),
        P("dp", "tensor"),
        P("dp", None, "tensor"),
        P("dp", None, "tensor"),
        P("dp", None, "tensor"),
        P("dp", None, "tensor"),
        P("dp", None, "tensor"),
        P("dp", None, "tensor"),
    )
    return jax.shard_map(
        per_device, mesh=mesh, in_specs=in_specs, out_specs=out_specs, check_vma=False
    )
```

profile of v0, /device:TPU:16, one launch (start us, length us, event | category | flops | bytes accessed | tf_op | source)
XLA Modules:
  0.0 247.5 jit_solution(7481131759192164001)
XLA Ops:
  7.2 1.7 convert_element_type.41
  9.0 0.7 fusion.28
  9.9 1.7 broadcast_multiply_fusion
  11.6 3.9 %fusion.43 = f32[2048,448]{0,1:T(8,128)} fusion(bf16[448,512]{1,0:T(8,128)(2,1)} %param.11, bf16[512,2048]{1,0:T(8,128)(2,1)S(1)} %copy-done), kind=kOutput, calls=%fused_computation.60 | convolution fusion | flops 939524096 | bytes 6225920 | tf_op jit(solution)/shard_map/dot_general | solution.py:83
  15.6 0.8 copy-done.4
  16.7 25.8 %all_gather.10 = bf16[448,8,128]{2,1,0:T(8,128)(2,1)S(1)} all-gather(bf16[14,8,128]{2,1,0:T(8,128)(2,1)S(1)} %convert_element_type.43), channel_id=1, replica_groups=mesh['dp'=32,'tensor'=16] {'dp'}, dimensions={0}, use_global_device_ids=true | all-gather | bytes 946176 | tf_op jit(solution)/shard_map/all_gather | solution.py:56
  42.5 0.3 fusion.3
  43.1 32.9 %all-gather.3.cloned.1.call-done = bf16[448,8,512]{2,1,0:T(8,128)(2,1)} async-done(((bf16[14,8,512]{2,1,0:T(8,128)(2,1)}), bf16[448,8,512]{2,1,0:T(8,128)(2,1)}) %all-gather.3.cloned.1.call-update) | async-done | bytes 3670032 | tf_op jit(solution)/shard_map/all_gather | solution.py:55
  75.9 4.1 %fusion = bf16[14,8,512]{2,0,1:T(8,128)(2,1)S(1)} fusion(bf16[448,8,512]{2,1,0:T(8,128)(2,1)} %all-gather.3.cloned.1.call-done, s32[14]{0:T(128)S(1)} %get-tuple-element.49), kind=kOutput, calls=%fused_computation | convolution fusion | flops 51386496 | bytes 3784760 | tf_op jit(solution)/shard_map/sc,crd->srd/dot_general | solution.py:62
  80.2 57.9 %all-reduce = (f32[14,32,8]{1,2,0:T(8,128)S(1)}, f32[14,32,8]{1,2,0:T(8,128)S(1)}) all-reduce(f32[14,32,8]{1,2,0:T(8,128)S(1)} %convolution_bitcast_fusion, f32[14,32,8]{1,2,0:T(8,128)S(1)} %fusion.15), channel_id=1, replica_groups=mesh['dp'=32,'tensor'=16] {'tensor'}, use_global_device_ids=true, to_apply=%region_1.2 | all-reduce | flops 7168 | bytes 57344 | tf_op jit(solution)/shard_map/psum | solution.py:79
  138.1 0.3 convolution_multiply_fusion.3
  138.4 0.3 fusion.18
  138.8 0.7 copy.93
  139.5 6.6 %all-to-all-start.1 = ((f32[32,8,128]{2,1,0:T(8,128)}), f32[32,8,128]{2,1,0:T(8,128)S(1)}, u32[]{:S(2)}, u32[]{:S(2)}) async-start(f32[32,8,128]{2,1,0:T(8,128)} %copy.93), calls=%async_computation.2 | async-start | bytes 262144 | tf_op jit(solution)/shard_map/all_to_all | solution.py:119
  146.1 0.3 convolution_multiply_fusion.1
  146.4 1.5 convolution_multiply_fusion
  147.9 7.8 %all-gather.5.cloned.1.call-done = bf16[448,2048]{1,0:T(8,128)(2,1)} async-done(((bf16[448,128]{1,0:T(8,128)(2,1)}), bf16[448,2048]{1,0:T(8,128)(2,1)}) %all-gather.5.cloned.1.call-update) | async-done | bytes 1835024 | tf_op jit(solution)/shard_map/all_gather | solution.py:98
  155.7 3.6 %fusion.2 = bf16[448,512]{1,0:T(8,128)(2,1)} fusion(f32[448,512]{1,0:T(8,128)} %bitcast.39, bf16[448,2048]{1,0:T(8,128)(2,1)} %all-gather.5.cloned.1.call-done, bf16[512,2048]{1,0:T(8,128)(2,1)S(1)} %copy-done), kind=kOutput, calls=%fused_computation.4 | convolution fusion | flops 939982848 | bytes 5308416 | tf_op jit(solution)/shard_map/dot_general | solution.py:97
  159.4 0.5 fusion.8
  159.9 1.1 copy.87
  161.0 8.4 %all-to-all-start = ((f32[32,8,512]{2,1,0:T(8,128)}), f32[32,8,512]{2,1,0:T(8,128)S(1)}, u32[]{:S(2)}, u32[]{:S(2)}) async-start(f32[32,8,512]{2,1,0:T(8,128)} %copy.87), calls=%async_computation.1 | async-start | bytes 1048576 | tf_op jit(solution)/shard_map/all_to_all | solution.py:118
  169.5 1.2 convolution_multiply_fusion.2
  170.7 1.1 copy_subtract_fusion.1
  171.8 0.6 copy.100
  172.4 0.6 copy.101
  173.1 0.6 copy.102
  173.7 61.1 %reduce-scatter.2.cloned.1.call-done = f32[128,448]{0,1:T(8,128)} async-done(((f32[2048,448]{0,1:T(8,128)}), f32[128,448]{0,1:T(8,128)}) %reduce-scatter.2.cloned.1.call-update) | async-done | bytes 229392 | tf_op jit(solution)/shard_map/reduce_scatter | solution.py:82
  234.8 1.6 fusion.11
  236.5 2.0 copy_subtract_fusion
  238.4 0.8 copy.97
  239.3 0.8 copy.98
  240.1 0.8 copy.99
  (34 shorter events, 1.1 us)
Async XLA Ops:
  7.2 4.4 %copy-start = (bf16[512,2048]{1,0:T(8,128)(2,1)S(1)}, bf16[512,2048]{1,0:T(8,128)(2,1)}, u32[]{:S(2)}) copy-start(bf16[512,2048]{1,0:T(8,128)(2,1)} %param.12) | copy-start | bytes 6291460
  7.2 68.7 %all-gather.3.cloned.1.call-start = ((), (), s32[]{:S(2)}) async-start(), calls=%async_computation.4 | async-start | bytes 3784704 | tf_op jit(solution)/shard_map/all_gather | solution.py:55
  9.0 146.7 %all-gather.5.cloned.1.call-start = ((), (), s32[]{:S(2)}) async-start(), calls=%async_computation.5 | async-start | bytes 1949696 | tf_op jit(solution)/shard_map/all_gather | solution.py:98
  11.6 223.3 %reduce-scatter.2.cloned.1.call-start = ((), (), s32[]{:S(2)}) async-start(), calls=%async_computation.3 | async-start | bytes 3899392 | tf_op jit(solution)/shard_map/reduce_scatter | solution.py:82
  15.6 0.8 copy-start.4
  15.6 0.8 copy-start.7
  15.6 26.9 %copy-start.8 = (s32[14]{0:T(128)S(1)}, s32[14]{0:T(128)}, u32[]{:S(2)}) copy-start(s32[14]{0:T(128)} %param.15) | copy-start | bytes 172
  15.6 27.2 %copy-start.5 = (bf16[448,128]{1,0:T(8,128)(2,1)S(1)}, bf16[448,128]{1,0:T(8,128)(2,1)}, u32[]{:S(2)}) copy-start(bf16[448,128]{1,0:T(8,128)(2,1)} %param.13) | copy-start | bytes 344068
  42.8 37.2 %copy-start.1 = (bf16[448,512]{1,0:T(8,128)(2,1)S(1)}, bf16[448,512]{1,0:T(8,128)(2,1)}, u32[]{:S(2)}) copy-start(bf16[448,512]{1,0:T(8,128)(2,1)} %param.11) | copy-start | bytes 1376260
  138.1 8.0 %copy-start.6 = (f32[14,32,8]{1,2,0:T(8,128)}, f32[14,32,8]{1,2,0:T(8,128)S(1)}, u32[]{:S(2)}) copy-start(f32[14,32,8]{1,2,0:T(8,128)S(1)} %get-tuple-element.40) | copy-start | bytes 43012
  139.5 21.5 %all-to-all-start.1 = ((f32[32,8,128]{2,1,0:T(8,128)}), f32[32,8,128]{2,1,0:T(8,128)S(1)}, u32[]{:S(2)}, u32[]{:S(2)}) async-start(f32[32,8,128]{2,1,0:T(8,128)} %copy.93), calls=%async_computation.2 | async-start | bytes 262144 | tf_op jit(solution)/shard_map/all_to_all | solution.py:119
  159.9 76.6 %copy-start.2 = (f32[14,8,512]{2,1,0:T(8,128)S(1)}, f32[14,8,512]{2,1,0:T(8,128)}, u32[]{:S(2)}) copy-start(f32[14,8,512]{2,1,0:T(8,128)} %param.16) | copy-start | bytes 688132
  159.9 76.6 %copy-start.3 = (f32[14,8,512]{2,1,0:T(8,128)S(1)}, f32[14,8,512]{2,1,0:T(8,128)}, u32[]{:S(2)}) copy-start(f32[14,8,512]{2,1,0:T(8,128)} %param.18) | copy-start | bytes 688132
  161.0 75.4 %all-to-all-start = ((f32[32,8,512]{2,1,0:T(8,128)}), f32[32,8,512]{2,1,0:T(8,128)S(1)}, u32[]{:S(2)}, u32[]{:S(2)}) async-start(f32[32,8,512]{2,1,0:T(8,128)} %copy.87), calls=%async_computation.1 | async-start | bytes 1048576 | tf_op jit(solution)/shard_map/all_to_all | solution.py:118
Sparse Core Ops, SparseCore 0:
  11.7 64.1 all-gather.2
  78.5 77.1 all-gather.4
  158.6 76.2 reduce-scatter.1
where the time goes:
time: 248 us; the launch traced here: 247 us
  waiting for transfers between devices  102 us (41%)
  blocking collectives  83.7 us (34%)
  matrix products  19.7 us (8%)
  starting transfers between devices  15.1 us (6%)
  between operations  13.9 us (6%)
  local copies, waits for them, and re-layouts  7.16 us (3%)
  other arithmetic  6.06 us (2%)
    reduce_scatter x1, waiting for transfers between devices, per_device(): lax.psum_scatter(lax.dot_general(weight, tokens, (((0,), (1,)), ((), ()))...  61.1 us
    psum x1, blocking collectives, per_device(): low_flat, up_flat = lax.psum((low_part, up_part), 'tensor')  57.9 us
    all_gather x1, waiting for transfers between devices, per_device(): lax.all_gather(down_half, 'dp', axis=0, tiled=True)  32.9 us
    all_gather x1, blocking collectives, per_device(): lax.all_gather(up_half, 'dp', axis=0, tiled=True)  25.8 us
    all_to_all x1, starting transfers between devices, per_device(): lax.all_to_all(send_grad_down, 'dp', split_axis=0, concat_axis=0, tiled=T...  8.41 us
    all_gather x1, waiting for transfers between devices, per_device(): lax.all_gather(cot_flat, 'tensor', axis=1, tiled=True)  7.78 us
    all_to_all x1, starting transfers between devices, per_device(): lax.all_to_all(send_grad_up, 'dp', split_axis=0, concat_axis=0, tiled=True)  6.58 us
    unnamed x24, local copies, waits for them, and re-layouts  5.23 us
  transfers between devices with their start and end apart: 5, of which 3 were waited for; matrix products, arithmetic and copies ran while one was open for 10% of the time, Pallas kernels for 0%

commit v1 on v0

v1 whole, which is shorter than its diff:
```python
import functools

import jax
import jax.numpy as jnp
from jax import lax
from jax.experimental import pallas as pl
from jax.experimental.pallas import tpu as pltpu
from jax.sharding import PartitionSpec as P

lowrank_scale = 2.0
learn_rate = 0.001
beta_first = 0.9
beta_second = 0.999
adam_eps = 1e-08
adam_step = 20.0
small_lag = 2
sum_lag = 5
MESH = pl.DeviceIdType.MESH


def adam_update(param, first, second, grad):
    new_first = beta_first * first + (1.0 - beta_first) * grad
    new_second = beta_second * second + (1.0 - beta_second) * grad * grad
    fix_first = 1.0 - beta_first**adam_step
    fix_second = 1.0 - beta_second**adam_step
    new_param = param - learn_rate * (new_first / fix_first) / (
        jnp.sqrt(new_second / fix_second) + adam_eps
    )
    return (new_param, new_first, new_second)


def dot(a, b, dims):
    return lax.dot_general(a, b, (dims, ((), ())), preferred_element_type=jnp.float32)


def dot_split(a, b, dims):
    high = a.astype(jnp.bfloat16)
    rest = (a - high.astype(jnp.float32)).astype(jnp.bfloat16)
    return dot(high, b, dims) + dot(rest, b, dims)


def step_kernel(
    n_dp,
    n_z,
    route_ref,
    count_ref,
    factor_ref,
    tok_ref,
    w_ref,
    cot_ref,
    ad_ref,
    au_ref,
    df_ref,
    ds_ref,
    uf_ref,
    us_ref,
    val_ref,
    tg_ref,
    nd_ref,
    ndf_ref,
    nds_ref,
    nu_ref,
    nuf_ref,
    nus_ref,
    send_a,
    recv_a,
    send_g,
    recv_g,
    slot_a,
    slot_g,
    ag,
    sm,
    part,
    out_r,
    in_r,
    out_l,
    in_l,
    back,
    sem_as,
    sem_ar,
    sem_gs,
    sem_gr,
    ag_rs,
    ag_rr,
    ag_ls,
    ag_lr,
    sm_rs,
    sm_rr,
    sm_ls,
    sm_lr,
    rs_rs,
    rs_rr,
    rs_ls,
    rs_lr,
):
    my_dp = lax.axis_index("dp")
    me = lax.axis_index("tensor")
    right = lax.rem(me + 1, n_z)
    left = lax.rem(me + n_z - 1, n_z)
    n_right = n_z // 2
    n_left = n_z - 1 - n_right
    slots, rank, width = ad_ref.shape
    cols = cot_ref.shape[1]
    rows = tok_ref.shape[0]
    block = rows // slots

    barrier = pltpu.get_barrier_semaphore()
    pl.semaphore_signal(barrier, inc=1, device_id={"tensor": right}, device_id_type=MESH)
    pl.semaphore_signal(barrier, inc=1, device_id={"tensor": left}, device_id_type=MESH)

    def greet(i, carry):
        other = lax.rem(my_dp + i, n_dp)
        pl.semaphore_signal(barrier, inc=1, device_id={"dp": other}, device_id_type=MESH)
        return carry

    lax.fori_loop(1, n_dp, greet, 0)

    def pack(g, carry):
        j = route_ref[0, g]
        send_a[g, :, :width] = ad_ref[j].astype(jnp.bfloat16)
        send_a[g, :, width:] = au_ref[j].astype(jnp.bfloat16)
        return carry

    lax.fori_loop(0, n_dp, pack, 0)
    at_row = lax.broadcasted_iota(jnp.int32, (block, cols), 0)
    for b in range(slots):
        here = pl.ds(b * block, block)
        ag[me, here, :] = jnp.where(
            at_row < count_ref[b], cot_ref[here, :].astype(jnp.float32), 0.0
        ).astype(jnp.bfloat16)

    pl.semaphore_wait(barrier, n_dp + 1)

    def adapter_copy(other, slot):
        return pltpu.make_async_remote_copy(
            src_ref=send_a.at[other],
            dst_ref=recv_a.at[slot],
            send_sem=sem_as.at[other],
            recv_sem=sem_ar.at[slot],
            device_id={"dp": other},
            device_id_type=MESH,
        )

    def grad_copy(other, slot):
        return pltpu.make_async_remote_copy(
            src_ref=send_g.at[other],
            dst_ref=recv_g.at[slot],
            send_sem=sem_gs.at[other],
            recv_sem=sem_gr.at[slot],
            device_id={"dp": other},
            device_id_type=MESH,
        )

    def every_other(action):
        def body(i, carry):
            action(lax.rem(my_dp + i, n_dp))
            return carry

        lax.fori_loop(1, n_dp, body, 0)

    def gather_copy(buf, sems, to_right, step):
        send_sem, recv_sem = sems
        owner = lax.rem(me + (n_z - step if to_right else step), n_z)
        return pltpu.make_async_remote_copy(
            src_ref=buf.at[owner],
            dst_ref=buf.at[owner],
            send_sem=send_sem.at[step],
            recv_sem=recv_sem.at[step],
            device_id={"tensor": right if to_right else left},
            device_id_type=MESH,
        )

    def gather_arrival(buf, sems, to_right, step):
        send_sem, recv_sem = sems
        owner = lax.rem(me + (2 * n_z - 1 - step if to_right else step + 1), n_z)
        pltpu.make_async_remote_copy(
            src_ref=buf.at[owner],
            dst_ref=buf.at[owner],
            send_sem=send_sem.at[step],
            recv_sem=recv_sem.at[step],
            device_id={"tensor": right if to_right else left},
            device_id_type=MESH,
        ).wait_recv()
        return owner

    def sum_copy(to_right, step):
        return pltpu.make_async_remote_copy(
            src_ref=(out_r if to_right else out_l).at[step],
            dst_ref=(in_r if to_right else in_l).at[step],
            send_sem=(rs_rs if to_right else rs_ls).at[step],
            recv_sem=(rs_rr if to_right else rs_lr).at[step],
            device_id={"tensor": right if to_right else left},
            device_id_type=MESH,
        )

    ag_right, ag_left = (ag_rs, ag_rr), (ag_ls, ag_lr)
    sm_right, sm_left = (sm_rs, sm_rr), (sm_ls, sm_lr)

    every_other(lambda other: adapter_copy(other, my_dp).start())
    gather_copy(ag, ag_right, True, 0).start()
    gather_copy(ag, ag_left, False, 0).start()
    recv_a[my_dp] = send_a[my_dp]

    def columns(c):
        return pl.ds(pl.multiple_of(c * cols, cols), cols)

    def forward(c, carry):
        part[c] = dot(tok_ref[...], w_ref[:, columns(c)], ((1,), (0,)))
        return carry

    lax.fori_loop(0, n_z, forward, 0)

    def backward(c, first=False):
        term = dot(ag[c], w_ref[:, columns(c)], ((1,), (1,)))
        back[...] = term if first else back[...] + term

    backward(me, True)

    of_slot = lax.broadcasted_iota(jnp.int32, (slots, rank, rows), 2) // block
    own_slot = of_slot == lax.broadcasted_iota(jnp.int32, (slots, rank, rows), 0)

    def fold(full):
        return jnp.sum(jnp.where(own_slot, full.reshape(slots, rank, rows), 0.0), axis=0)

    def unfold(ranks):
        return jnp.where(own_slot, ranks[None], 0.0).reshape(slots * rank, rows)

    def small_begin():
        every_other(lambda other: adapter_copy(my_dp, other).wait_recv())
        for b in range(slots):
            slot_a[b * rank : (b + 1) * rank, :] = recv_a[route_ref[1, b]].astype(jnp.float32)
        own = slot_a[...].astype(jnp.bfloat16)
        sm[me, :rank, :] = fold(dot(own[:, :width], tok_ref[...], ((1,), (1,))))
        sm[me, rank:, :] = fold(dot(own[:, width:], ag[me], ((1,), (1,))))
        gather_copy(sm, sm_right, True, 0).start()
        gather_copy(sm, sm_left, False, 0).start()

    def small_end():
        total = sm[0]
        for c in range(1, n_z):
            total = total + sm[c]
        low = unfold(total[:rank])
        up = unfold(total[rank:])
        grads = (
            dot_split(up, tok_ref[...], ((1,), (0,))),
            dot_split(low, ag[me], ((1,), (0,))),
        )
        for b in range(slots):
            for grad, at in zip(grads, (pl.ds(0, width), pl.ds(width, cols))):
                slot_g[b, :, at] = factor_ref[b] * grad[b * rank : (b + 1) * rank]

        def pack_grad(g, carry):
            send_g[g] = slot_g[route_ref[2, g]]
            return carry

        lax.fori_loop(0, n_dp, pack_grad, 0)
        every_other(lambda other: grad_copy(other, my_dp).start())
        recv_g[my_dp] = send_g[my_dp]
        own = slot_a[...].astype(jnp.bfloat16)
        back[...] += lowrank_scale * dot_split(up, own[:, :width], ((0,), (0,)))
        part[me] += lowrank_scale * dot_split(low, own[:, width:], ((0,), (0,)))

    def update():
        every_other(lambda other: grad_copy(my_dp, other).wait_recv())

        def one(j, carry):
            grad = recv_g[route_ref[3, j]]
            nd_ref[j], ndf_ref[j], nds_ref[j] = adam_update(
                ad_ref[j], df_ref[j], ds_ref[j], grad[:, :width]
            )
            nu_ref[j], nuf_ref[j], nus_ref[j] = adam_update(
                au_ref[j], uf_ref[j], us_ref[j], grad[:, width:]
            )
            return carry

        lax.fori_loop(0, slots, one, 0)

    def sum_send(step):
        for to_right, out, arrived, last in (
            (True, out_r, in_r, n_right),
            (False, out_l, in_l, n_left),
        ):
            if step > last:
                continue
            if step > 0:
                sum_copy(to_right, step - 1).wait_recv()
            if step < last:
                ahead = last - step
                c = lax.rem(me + (ahead if to_right else n_z - ahead), n_z)
                term = part[c]
                if step > 0:
                    term = term + arrived[step - 1]
                out[step] = term
                sum_copy(to_right, step).start()

    for t in range(max(n_right + sum_lag + 1, n_right + small_lag + 2)):
        if t < n_right:
            for to_right, sems, last in ((True, ag_right, n_right), (False, ag_left, n_left)):
                if t < last:
                    owner = gather_arrival(ag, sems, to_right, t)
                    if t + 1 < last:
                        gather_copy(ag, sems, to_right, t + 1).start()
                    backward(owner)
        s = t - small_lag
        if s == 0:
            small_begin()
        if 0 < s <= n_right:
            for to_right, sems, last in ((True, sm_right, n_right), (False, sm_left, n_left)):
                if s - 1 < last:
                    gather_arrival(sm, sems, to_right, s - 1)
                    if s < last:
                        gather_copy(sm, sems, to_right, s).start()
        s = t - sum_lag
        if 0 <= s <= n_right:
            sum_send(s)
        if t - small_lag == n_right:
            small_end()
        if t == n_right + small_lag + 2:
            update()
    if n_right + small_lag + 2 >= max(n_right + sum_lag + 1, n_right + small_lag + 2):
        update()

    tg_ref[...] = back[...].astype(jnp.bfloat16)
    val_ref[...] = (part[me] + in_r[n_right - 1] + in_l[n_left - 1]).astype(jnp.bfloat16)

    every_other(lambda other: adapter_copy(other, my_dp).wait_send())
    every_other(lambda other: grad_copy(other, my_dp).wait_send())
    for to_right, last in ((True, n_right), (False, n_left)):
        for step in range(last):
            gather_copy(ag, ag_right if to_right else ag_left, to_right, step).wait_send()
            gather_copy(sm, sm_right if to_right else sm_left, to_right, step).wait_send()
            sum_copy(to_right, step).wait_send()


def per_device(
    tokens,
    weight,
    cotangent,
    slot_job,
    slot_count,
    adapter_down,
    adapter_up,
    down_first,
    down_second,
    up_first,
    up_second,
):
    n_dp = lax.axis_size("dp")
    n_z = lax.axis_size("tensor")
    slots, rank, width = adapter_down.shape
    cols = adapter_up.shape[2]
    rows = tokens.shape[0]
    group = lax.axis_index("dp")
    groups = jnp.arange(n_dp, dtype=jnp.int32)
    local = jnp.arange(slots, dtype=jnp.int32)
    my_jobs = lax.dynamic_slice_in_dim(slot_job, group * slots, slots)
    owner = my_jobs // slots
    job_group = slot_job.reshape(n_dp, slots)
    match = job_group[:, :, None] == (group * slots + local)[None, None, :]
    here = jnp.any(match, axis=1)
    job_for_group = jnp.sum(jnp.where(here, local[None, :], 0), axis=1)
    group_of_job = jnp.sum(jnp.where(here, groups[:, None], 0), axis=0)
    slot_for_owner = jnp.sum(
        jnp.where(owner[None, :] == groups[:, None], local[None, :], 0), axis=1
    )
    pad = (0, n_dp - slots)
    route = jnp.stack(
        [job_for_group, jnp.pad(owner, pad), slot_for_owner, jnp.pad(group_of_job, pad)]
    ).astype(jnp.int32)
    factor = lowrank_scale / slot_count.astype(jnp.float32)

    smem = pl.BlockSpec(memory_space=pltpu.SMEM)
    vmem = pl.BlockSpec(memory_space=pltpu.VMEM)
    n_right = n_z // 2
    n_left = n_z - 1 - n_right
    f32, bf16 = jnp.float32, jnp.bfloat16
    dma = pltpu.SemaphoreType.DMA
    down = jax.ShapeDtypeStruct(adapter_down.shape, f32)
    up = jax.ShapeDtypeStruct(adapter_up.shape, f32)
    ring_sems = [dma((n_right,)), dma((n_right,)), dma((n_left,)), dma((n_left,))]
    return pl.pallas_call(
        functools.partial(step_kernel, n_dp, n_z),
        out_shape=(
            jax.ShapeDtypeStruct(cotangent.shape, bf16),
            jax.ShapeDtypeStruct(tokens.shape, bf16),
            down,
            down,
            down,
            up,
            up,
            up,
        ),
        in_specs=[smem] * 3 + [vmem] * 9,
        out_specs=(vmem,) * 8,
        scratch_shapes=[
            pltpu.VMEM((n_dp, rank, width + cols), bf16),
            pltpu.VMEM((n_dp, rank, width + cols), bf16),
            pltpu.VMEM((n_dp, rank, width + cols), f32),
            pltpu.VMEM((n_dp, rank, width + cols), f32),
            pltpu.VMEM((slots * rank, width + cols), f32),
            pltpu.VMEM((slots, rank, width + cols), f32),
            pltpu.VMEM((n_z, rows, cols), bf16),
            pltpu.VMEM((n_z, 2 * rank, rows), f32),
            pltpu.VMEM((n_z, rows, cols), f32),
            pltpu.VMEM((n_right, rows, cols), f32),
            pltpu.VMEM((n_right, rows, cols), f32),
            pltpu.VMEM((n_left, rows, cols), f32),
            pltpu.VMEM((n_left, rows, cols), f32),
            pltpu.VMEM((rows, width), f32),
            dma((n_dp,)),
            dma((n_dp,)),
            dma((n_dp,)),
            dma((n_dp,)),
        ]
        + ring_sems * 3,
        compiler_params=pltpu.CompilerParams(collective_id=0, has_side_effects=True),
        name="adapter_step",
    )(
        route,
        slot_count,
        factor,
        tokens,
        weight,
        cotangent,
        adapter_down,
        adapter_up,
        down_first,
        down_second,
        up_first,
        up_second,
    )


def solution(mesh):
    in_specs = (
        P("dp", "tensor"),
        P("tensor", None),
        P("dp", "tensor"),
        P(),
        P("dp"),
        P("dp", None, "tensor"),
        P("dp", None, "tensor"),
        P("dp", None, "tensor"),
        P("dp", None, "tensor"),
        P("dp", None, "tensor"),
        P("dp", None, "tensor"),
    )
    out_specs = (
        P("dp", "tensor"),
        P("dp", "tensor"),
        P("dp", None, "tensor"),
        P("dp", None, "tensor"),
        P("dp", None, "tensor"),
        P("dp", None, "tensor"),
        P("dp", None, "tensor"),
        P("dp", None, "tensor"),
    )
    return jax.shard_map(
        per_device, mesh=mesh, in_specs=in_specs, out_specs=out_specs, check_vma=False
    )
```

time: 248 us -> 117 us (0.47)
  the two profiles are of different devices: /device:TPU:16 before, /device:TPU:8 now
where the time goes in v1:
time: 117 us
  Pallas kernels  104 us (89%)
  local copies, waits for them, and re-layouts  10.1 us (9%)
  other arithmetic  2.85 us (2%)
    pallas_call x1, Pallas kernels, per_device(): pl.pallas_call(functools.partial(step_kernel, n_dp, n_z), out_shape=(jax....  104 us
    unnamed x16, local copies, waits for them, and re-layouts  9.27 us

profile of v1, /device:TPU:8, one launch (start us, length us, event | category | flops | bytes accessed | tf_op | source)
XLA Modules:
  0.0 117.2 jit_solution(9130978956221724308)
XLA Ops:
  0.6 0.8 and_select_fusion
  1.4 0.1 select_reduce_fusion.1
  1.5 1.2 %convert_divide_fusion.factor_ref = f32[14]{0:T(128)} fusion(s32[14]{0:T(128)} %count_ref.1), kind=kLoop, calls=%fused_computation.7 | loop fusion | flops 28 | bytes 112 | tf_op jit(solution)/shard_map/div | solution.py:370
  2.7 0.8 eq.30
  3.5 0.1 copy.19
  3.5 0.1 compare_reduce_fusion
  3.6 0.1 select_reduce_fusion.2
  3.8 0.6 pad_add_fusion.route_ref
  4.4 103.5 %adapter_step.1 = (bf16[448,128]{1,0:T(8,128)(2,1)}, bf16[448,512]{1,0:T(8,128)(2,1)}, f32[14,8,512]{2,1,0:T(8,128)}, f32[14,8,512]{2,1,0:T(8,128)}, f32[14,8,51...) custom-call(s32[4,32]{1,0:T(4,128)} %pad_add_fusion.route_ref, ...), custom_call_target="tpu_custom_call" | custom-call | tf_op jit(solution)/shard_map/adapter_step/pallas_call | solution.py:381
  107.9 0.0 copy-start
  107.9 0.0 copy-start.3
  107.9 0.0 copy-start.2
  107.9 0.0 copy-start.1
  107.9 1.6 %copy.28 = bf16[448,128]{1,0:T(8,128)(2,1)} copy(bf16[448,128]{1,0:T(8,128)(2,1)} %get-tuple-element.20) | data formatting | bytes 229376
  109.5 1.8 %copy.29 = bf16[448,512]{1,0:T(8,128)(2,1)} copy(bf16[448,512]{1,0:T(8,128)(2,1)} %get-tuple-element.21) | data formatting | bytes 917504
  111.3 1.6 %copy.30 = f32[14,8,512]{2,1,0:T(8,128)} copy(f32[14,8,512]{2,1,0:T(8,128)} %get-tuple-element.22) | data formatting | bytes 458752
  113.0 1.6 %copy.31 = f32[14,8,512]{2,1,0:T(8,128)} copy(f32[14,8,512]{2,1,0:T(8,128)} %get-tuple-element.23) | data formatting | bytes 458752
  114.6 0.0 copy-done
  114.6 0.7 copy.32
  115.3 0.0 copy-done.3
  115.3 0.6 copy.33
  115.9 0.0 copy-done.2
  115.9 0.6 copy.34
  116.6 0.0 copy-done.1
  116.6 0.6 copy.35
  (2 shorter events, 0.0 us)
Async XLA Ops:
  107.9 6.7 %copy-start = (f32[14,8,512]{2,1,0:T(8,128)S(1)}, f32[14,8,512]{2,1,0:T(8,128)}, u32[]{:S(2)}) copy-start(f32[14,8,512]{2,1,0:T(8,128)} %get-tuple-element.24) | copy-start | bytes 688132
  107.9 7.4 %copy-start.3 = (f32[14,8,128]{2,1,0:T(8,128)S(1)}, f32[14,8,128]{2,1,0:T(8,128)}, u32[]{:S(2)}) copy-start(f32[14,8,128]{2,1,0:T(8,128)} %get-tuple-element.25) | copy-start | bytes 172036
  107.9 8.0 %copy-start.2 = (f32[14,8,128]{2,1,0:T(8,128)S(1)}, f32[14,8,128]{2,1,0:T(8,128)}, u32[]{:S(2)}) copy-start(f32[14,8,128]{2,1,0:T(8,128)} %get-tuple-element.26) | copy-start | bytes 172036
  107.9 8.7 %copy-start.1 = (f32[14,8,128]{2,1,0:T(8,128)S(1)}, f32[14,8,128]{2,1,0:T(8,128)}, u32[]{:S(2)}) copy-start(f32[14,8,128]{2,1,0:T(8,128)} %get-tuple-element.27) | copy-start | bytes 172036

commit v2 on v1

v2 whole, which is shorter than its diff:
```python
import functools

import jax
import jax.numpy as jnp
from jax import lax
from jax.experimental import pallas as pl
from jax.experimental.pallas import tpu as pltpu
from jax.sharding import PartitionSpec as P

lowrank_scale = 2.0
learn_rate = 0.001
beta_first = 0.9
beta_second = 0.999
adam_eps = 1e-08
adam_step = 20.0
small_lag = 1
sum_lag = 4
ln2 = 0.6931471805599453
inv_ln2 = 1.4426950408889634
code_bits = 14.0
code_rows = 16
MESH = pl.DeviceIdType.MESH


def adam_update(param, first, second, grad):
    new_first = beta_first * first + (1.0 - beta_first) * grad
    new_second = beta_second * second + (1.0 - beta_second) * grad * grad
    fix_first = 1.0 - beta_first**adam_step
    fix_second = 1.0 - beta_second**adam_step
    new_param = param - learn_rate * (new_first / fix_first) / (
        jnp.sqrt(new_second / fix_second) + adam_eps
    )
    return (new_param, new_first, new_second)


def dot(a, b, dims):
    return lax.dot_general(a, b, (dims, ((), ())), preferred_element_type=jnp.float32)


def dot_split(a, b, dims):
    high = a.astype(jnp.bfloat16)
    rest = (a - high.astype(jnp.float32)).astype(jnp.bfloat16)
    return dot(high, b, dims) + dot(rest, b, dims)


def encode(x, rows):
    top = jnp.max(jnp.abs(x), axis=0, keepdims=True)
    power = jnp.ceil(jnp.log(jnp.maximum(top, 1e-28)) * inv_ln2)
    fixed = jnp.round(x * jnp.exp((code_bits - power) * ln2)).astype(jnp.int32)
    tail = jnp.broadcast_to(power, (code_rows, x.shape[1])).astype(jnp.int32)
    return fixed.astype(jnp.int16), tail.astype(jnp.int16)


def decode(ref, rows):
    power = ref[rows:, :].astype(jnp.int32).astype(jnp.float32)[:1]
    return ref[:rows, :].astype(jnp.int32).astype(jnp.float32) * jnp.exp(
        (power - code_bits) * ln2
    )


def step_kernel(
    n_dp,
    n_z,
    job_ref,
    count_ref,
    to_group_ref,
    to_owner_ref,
    group_ref,
    tok_hbm,
    w_hbm,
    cot_ref,
    ad_ref,
    au_ref,
    val_ref,
    tg_ref,
    grad_ref,
    tok_ref,
    w_ref,
    send_a,
    recv_a,
    send_g,
    recv_g,
    slot_a,
    slot_g,
    ag,
    sm,
    part,
    sum_out,
    sum_in,
    back,
    load_sem,
    sem_as,
    sem_ar,
    sem_gs,
    sem_gr,
    ag_s,
    ag_r,
    sm_s,
    sm_r,
    rs_s,
    rs_r,
):
    my_dp = lax.axis_index("dp")
    me = lax.axis_index("tensor")
    right = lax.rem(me + 1, n_z)
    left = lax.rem(me + n_z - 1, n_z)
    hops = n_z // 2
    slots, rank, width = ad_ref.shape
    cols = cot_ref.shape[1]
    rows = cot_ref.shape[0]
    half = rows // 2
    block = rows // slots

    load_w = pltpu.make_async_copy(w_hbm, w_ref, load_sem.at[0])
    load_tok = pltpu.make_async_copy(tok_hbm, tok_ref, load_sem.at[1])
    load_tok.start()
    load_w.start()

    barrier = pltpu.get_barrier_semaphore()
    pl.semaphore_signal(barrier, inc=1, device_id={"tensor": right}, device_id_type=MESH)
    pl.semaphore_signal(barrier, inc=1, device_id={"tensor": left}, device_id_type=MESH)

    def greet(i, carry):
        other = lax.rem(my_dp + i, n_dp)
        pl.semaphore_signal(barrier, inc=1, device_id={"dp": other}, device_id_type=MESH)
        return carry

    lax.fori_loop(1, n_dp, greet, 0)

    at_row = lax.broadcasted_iota(jnp.int32, (block, cols), 0)
    for b in range(slots):
        here = pl.ds(b * block, block)
        ag[me, here, :] = jnp.where(
            at_row < count_ref[b], cot_ref[here, :].astype(jnp.float32), 0.0
        ).astype(jnp.bfloat16)

    def pack(g, carry):
        j = to_group_ref[g]
        send_a[g, :, :width] = ad_ref[j].astype(jnp.bfloat16)
        send_a[g, :, width:] = au_ref[j].astype(jnp.bfloat16)
        return carry

    lax.fori_loop(0, n_dp, pack, 0)
    pl.semaphore_wait(barrier, n_dp + 1)

    def adapter_copy(other, slot):
        return pltpu.make_async_remote_copy(
            src_ref=send_a.at[other],
            dst_ref=recv_a.at[slot],
            send_sem=sem_as.at[other],
            recv_sem=sem_ar.at[slot],
            device_id={"dp": other},
            device_id_type=MESH,
        )

    def grad_copy(other, slot):
        return pltpu.make_async_remote_copy(
            src_ref=send_g.at[other],
            dst_ref=recv_g.at[slot],
            send_sem=sem_gs.at[other],
            recv_sem=sem_gr.at[slot],
            device_id={"dp": other},
            device_id_type=MESH,
        )

    def every_other(action):
        def body(i, carry):
            action(lax.rem(my_dp + i, n_dp))
            return carry

        lax.fori_loop(1, n_dp, body, 0)

    streams = [(0, True), (1, False), (0, False), (1, True)]

    def length(stream):
        h, to_right = stream
        return hops if (h == 0) == to_right else hops - 1

    def index(stream):
        return stream[0] * 2 + int(stream[1])

    def ring_copy(buf, size, sems, stream, step, arriving):
        h, to_right = stream
        back_by = step + 1 if arriving else step
        owner = lax.rem(me + (2 * n_z - back_by if to_right else back_by), n_z)
        place = buf.at[owner, pl.ds(h * size, size), :]
        return pltpu.make_async_remote_copy(
            src_ref=place,
            dst_ref=place,
            send_sem=sems[0].at[index(stream), step],
            recv_sem=sems[1].at[index(stream), step],
            device_id={"tensor": right if to_right else left},
            device_id_type=MESH,
        )

    def gather(step, stream, arriving=False):
        return ring_copy(ag, half, (ag_s, ag_r), stream, step, arriving)

    def small(step, stream, arriving=False):
        return ring_copy(sm, rank, (sm_s, sm_r), stream, step, arriving)

    def relay(ring, step):
        for stream in streams:
            if step < length(stream):
                ring(step, stream, True).wait_recv()
                if step + 1 < length(stream):
                    ring(step + 1, stream).start()

    def sum_copy(step, stream):
        i = index(stream)
        return pltpu.make_async_remote_copy(
            src_ref=sum_out.at[i, step],
            dst_ref=sum_in.at[i, step],
            send_sem=rs_s.at[i, step],
            recv_sem=rs_r.at[i, step],
            device_id={"tensor": right if stream[1] else left},
            device_id_type=MESH,
        )

    def columns(c):
        return pl.ds(pl.multiple_of(c * cols, cols), cols)

    def chunk(offset):
        return lax.rem(me + n_z + offset, n_z)

    def forward(offsets):
        w = [w_ref[:, columns(chunk(o))] for o in offsets]
        w = w[0] if len(w) == 1 else jnp.concatenate(w, axis=1)
        product = dot(tok_ref[...], w, ((1,), (0,)))
        for i, o in enumerate(offsets):
            part[chunk(o)] = product[:, i * cols : (i + 1) * cols]

    def forward_for(step):
        ahead = hops - step
        forward([ahead, -ahead] if 0 < ahead < hops else [ahead])

    def backward(offsets, first=False):
        cot = [ag[chunk(o)] for o in offsets]
        w = [w_ref[:, columns(chunk(o))] for o in offsets]
        cot = cot[0] if len(cot) == 1 else jnp.concatenate(cot, axis=1)
        w = w[0] if len(w) == 1 else jnp.concatenate(w, axis=1)
        term = dot(cot, w, ((1,), (1,)))
        back[...] = term if first else back[...] + term

    def sum_step(step):
        for stream in streams:
            start = hops - length(stream)
            if step < start:
                continue
            h, to_right = stream
            i = index(stream)
            here = pl.ds(h * half, half)
            ahead = hops - step
            c = chunk(ahead if to_right else -ahead)
            total = part[c, here, :]
            if step > start:
                sum_copy(step - 1, stream).wait_recv()
                total = total + decode(sum_in.at[i, step - 1], half)
            if step == hops:
                part[c, here, :] = total
                continue
            sum_out[i, step, :half, :], sum_out[i, step, half:, :] = encode(total, half)
            sum_copy(step, stream).start()

    of_slot = lax.broadcasted_iota(jnp.int32, (slots, rank, rows), 2) // block
    own_slot = of_slot == lax.broadcasted_iota(jnp.int32, (slots, rank, rows), 0)

    def fold(full):
        return jnp.sum(jnp.where(own_slot, full.reshape(slots, rank, rows), 0.0), axis=0)

    def unfold(ranks):
        return jnp.where(own_slot, ranks[None], 0.0).reshape(slots * rank, rows)

    def small_begin():
        every_other(lambda other: adapter_copy(my_dp, other).wait_recv())
        for b in range(slots):
            owner = job_ref[my_dp * slots + b] // slots
            slot_a[b * rank : (b + 1) * rank, :] = recv_a[owner].astype(jnp.float32)
        own = slot_a[...].astype(jnp.bfloat16)
        sm[me, :rank, :] = fold(dot(own[:, :width], tok_ref[...], ((1,), (1,))))
        sm[me, rank:, :] = fold(dot(own[:, width:], ag[me], ((1,), (1,))))
        for stream in streams:
            small(0, stream).start()

    def small_end():
        total = sm[0]
        for c in range(1, n_z):
            total = total + sm[c]
        low = unfold(total[:rank])
        up = unfold(total[rank:])
        grads = (
            dot_split(up, tok_ref[...], ((1,), (0,))),
            dot_split(low, ag[me], ((1,), (0,))),
        )
        for b in range(slots):
            count = jnp.full((rank, cols), count_ref[b], jnp.int32).astype(jnp.float32)
            factor = (lowrank_scale / count)[:, :1]
            for grad, at in zip(grads, (pl.ds(0, width), pl.ds(width, cols))):
                slot_g[b, :, at] = factor * grad[b * rank : (b + 1) * rank]

        def pack_grad(g, carry):
            send_g[g] = slot_g[to_owner_ref[g]]
            return carry

        lax.fori_loop(0, n_dp, pack_grad, 0)
        every_other(lambda other: grad_copy(other, my_dp).start())
        recv_g[my_dp] = send_g[my_dp]
        return low, up

    def low_rank_terms(low, up):
        own = slot_a[...].astype(jnp.bfloat16)
        back[...] += lowrank_scale * dot_split(up, own[:, :width], ((0,), (0,)))
        part[me] += lowrank_scale * dot_split(low, own[:, width:], ((0,), (0,)))

    for stream in streams:
        gather(0, stream).start()
    every_other(lambda other: adapter_copy(other, my_dp).start())
    recv_a[my_dp] = send_a[my_dp]
    load_tok.wait()
    load_w.wait()
    forward_for(0)
    backward([0], True)

    for t in range(max(hops + sum_lag, hops + small_lag) + 1):
        s = t - small_lag
        if 0 < s <= hops:
            relay(small, s - 1)
        if t < hops:
            relay(gather, t)
        u = t - sum_lag
        if 0 <= u <= hops:
            sum_step(u)
        if s == 0:
            small_begin()
        if s == hops:
            low, up = small_end()
        if t < hops:
            backward([-1 - t, 1 + t] if t + 1 < hops else [hops])
        if t < hops:
            forward_for(t + 1)
        if s == hops:
            low_rank_terms(low, up)

    tg_ref[...] = back[...].astype(jnp.bfloat16)
    val_ref[...] = part[me].astype(jnp.bfloat16)
    every_other(lambda other: grad_copy(my_dp, other).wait_recv())

    def take(j, carry):
        grad_ref[j] = recv_g[group_ref[j] // slots]
        return carry

    lax.fori_loop(0, slots, take, 0)
    every_other(lambda other: adapter_copy(other, my_dp).wait_send())
    every_other(lambda other: grad_copy(other, my_dp).wait_send())
    for stream in streams:
        for step in range(length(stream)):
            gather(step, stream).wait_send()
            small(step, stream).wait_send()
            sum_copy(step + hops - length(stream), stream).wait_send()


def finish_kernel(
    val_ref,
    tg_ref,
    grad_ref,
    ad_ref,
    au_ref,
    df_ref,
    ds_ref,
    uf_ref,
    us_ref,
    val_out,
    tg_out,
    nd_ref,
    ndf_ref,
    nds_ref,
    nu_ref,
    nuf_ref,
    nus_ref,
):
    width = ad_ref.shape[2]
    val_out[...] = val_ref[...]
    tg_out[...] = tg_ref[...]
    for j in range(ad_ref.shape[0]):
        nd_ref[j], ndf_ref[j], nds_ref[j] = adam_update(
            ad_ref[j], df_ref[j], ds_ref[j], grad_ref[j, :, :width]
        )
        nu_ref[j], nuf_ref[j], nus_ref[j] = adam_update(
            au_ref[j], uf_ref[j], us_ref[j], grad_ref[j, :, width:]
        )


def per_device(
    tokens,
    weight,
    cotangent,
    slot_job,
    slot_count,
    adapter_down,
    adapter_up,
    down_first,
    down_second,
    up_first,
    up_second,
):
    n_dp = lax.axis_size("dp")
    n_z = lax.axis_size("tensor")
    slots, rank, width = adapter_down.shape
    cols = adapter_up.shape[2]
    rows = tokens.shape[0]
    group = lax.axis_index("dp")
    groups = jnp.arange(n_dp, dtype=jnp.int32)
    local = jnp.arange(slots, dtype=jnp.int32)
    my_jobs = lax.dynamic_slice_in_dim(slot_job, group * slots, slots)
    to_owner = jnp.sum(
        jnp.where((my_jobs // slots)[None, :] == groups[:, None], local[None, :], 0), axis=1
    )
    match = slot_job[None, :] == (group * slots + local)[:, None]
    all_slots = jnp.arange(slot_job.shape[0], dtype=jnp.int32)
    job_place = jnp.sum(jnp.where(match, all_slots[None, :], 0), axis=1)
    to_group = jnp.sum(
        jnp.where((job_place // slots)[None, :] == groups[:, None], local[None, :], 0), axis=1
    )

    smem = pl.BlockSpec(memory_space=pltpu.SMEM)
    vmem = pl.BlockSpec(memory_space=pltpu.VMEM)
    whole = pl.BlockSpec(memory_space=pl.ANY)
    hops = n_z // 2
    f32, bf16 = jnp.float32, jnp.bfloat16
    dma = pltpu.SemaphoreType.DMA
    shape = jax.ShapeDtypeStruct
    both = width + cols
    coded = (4, hops, rows // 2 + code_rows, cols)
    values, token_grad, grads = pl.pallas_call(
        functools.partial(step_kernel, n_dp, n_z),
        out_shape=(
            shape(cotangent.shape, bf16),
            shape(tokens.shape, bf16),
            shape((slots, rank, both), f32),
        ),
        in_specs=[smem] * 5 + [whole] * 2 + [vmem] * 3,
        out_specs=(vmem,) * 3,
        scratch_shapes=[
            pltpu.VMEM(tokens.shape, bf16),
            pltpu.VMEM(weight.shape, bf16),
            pltpu.VMEM((n_dp, rank, both), bf16),
            pltpu.VMEM((n_dp, rank, both), bf16),
            pltpu.VMEM((n_dp, rank, both), f32),
            pltpu.VMEM((n_dp, rank, both), f32),
            pltpu.VMEM((slots * rank, both), f32),
            pltpu.VMEM((slots, rank, both), f32),
            pltpu.VMEM((n_z, rows, cols), bf16),
            pltpu.VMEM((n_z, 2 * rank, rows), f32),
            pltpu.VMEM((n_z, rows, cols), f32),
            pltpu.VMEM(coded, jnp.int16),
            pltpu.VMEM(coded, jnp.int16),
            pltpu.VMEM((rows, width), f32),
            dma((2,)),
        ]
        + [dma((n_dp,))] * 4
        + [dma((4, hops))] * 6,
        compiler_params=pltpu.CompilerParams(collective_id=0, has_side_effects=True),
        name="adapter_step",
    )(
        slot_job,
        slot_count,
        to_group,
        to_owner,
        job_place,
        tokens,
        weight,
        cotangent,
        adapter_down,
        adapter_up,
    )
    down = shape(adapter_down.shape, f32)
    up = shape(adapter_up.shape, f32)
    return pl.pallas_call(
        finish_kernel,
        out_shape=(
            shape(values.shape, bf16),
            shape(token_grad.shape, bf16),
            down,
            down,
            down,
            up,
            up,
            up,
        ),
        in_specs=[vmem] * 9,
        out_specs=(vmem,) * 8,
        name="finish",
    )(
        values,
        token_grad,
        grads,
        adapter_down,
        adapter_up,
        down_first,
        down_second,
        up_first,
        up_second,
    )


def solution(mesh):
    in_specs = (
        P("dp", "tensor"),
        P("tensor", None),
        P("dp", "tensor"),
        P(),
        P("dp"),
        P("dp", None, "tensor"),
        P("dp", None, "tensor"),
        P("dp", None, "tensor"),
        P("dp", None, "tensor"),
        P("dp", None, "tensor"),
        P("dp", None, "tensor"),
    )
    out_specs = (
        P("dp", "tensor"),
        P("dp", "tensor"),
        P("dp", None, "tensor"),
        P("dp", None, "tensor"),
        P("dp", None, "tensor"),
        P("dp", None, "tensor"),
        P("dp", None, "tensor"),
        P("dp", None, "tensor"),
    )
    return jax.shard_map(
        per_device, mesh=mesh, in_specs=in_specs, out_specs=out_specs, check_vma=False
    )
```

time: 117 us -> 84.5 us (0.72)
  Pallas kernels: 104 us -> 81.4 us
  local copies, waits for them, and re-layouts: 10.1 us -> 0.01 us
    pallas_call x1 -> x2, Pallas kernels: 104 us -> 81.4 us  [the longest x1 78.8 us: per_device(): pl.pallas_call(functools.partial(step_kernel, n_dp, n_z), out_shape=(shap...]
    unnamed x16 -> x2, local copies, waits for them, and re-layouts: 9.27 us -> 0.01 us
    reduce_sum x2, other arithmetic: 0.21 us -> 1.47 us  [the longest x1 0.87 us: per_device(): job_place = jnp.sum(jnp.where(match, all_slots[None, :], 0), axis=1)]
    div x1 -> x0, other arithmetic: 1.17 us -> none  [per_device(): factor = lowrank_scale / slot_count.astype(jnp.float32)]
where the time goes in v2:
time: 84.5 us; the launch traced here: 84.3 us
  Pallas kernels  81.4 us (96%)
  other arithmetic  2.26 us (3%)
    pallas_call x1, Pallas kernels, per_device(): pl.pallas_call(functools.partial(step_kernel, n_dp, n_z), out_shape=(shap...  78.8 us
    pallas_call x1, Pallas kernels, per_device(): pl.pallas_call(finish_kernel, out_shape=(shape(values.shape, bf16), shape...  2.57 us

profile of v2, /device:TPU:8, one launch (start us, length us, event | category | flops | bytes accessed | tf_op | source)
XLA Modules:
  0.0 84.3 jit_solution(9162474539943435346)
XLA Ops:
  0.6 0.8 and_select_fusion
  1.4 0.9 %select_reduce_fusion.group_ref = s32[14]{0:T(128)S(1)} fusion(s32[448]{0:T(512)} %job_ref.1, s32[14]{0:T(128)S(1)} %iota_add_fusion), kind=kLoop, calls=%fused_computation | loop fusion | flops 18802 | bytes 1904 | tf_op jit(solution)/shard_map/reduce_sum | solution.py:420
  2.3 0.0 copy-start
  2.3 0.6 select_reduce_fusion.1
  2.9 0.0 copy-done
  2.9 78.8 %adapter_step.1 = (bf16[448,128]{1,0:T(8,128)(2,1)}, bf16[448,512]{1,0:T(8,128)(2,1)}, f32[14,8,640]{2,1,0:T(8,128)}) custom-call(s32[448]{0:T(512)} %job_ref.1, s32[14]{0:T(128)} %count_ref.1, s32[32]{0:T(128)} %get-tuple-element.15.to_group_ref, s32[32]{0:T(128)} %get-tuple-element.14.to_owner_ref, s32[14]{0:T(128)} %copy-done, bf16[448,512]{1,0:T(8,128)(2,1)} %tok_hbm.1, ...), custom_call_target="tpu_custom_call" | custom-call | tf_op jit(solution)/shard_map/adapter_step/pallas_call | solution.py:434
  81.7 2.6 %finish.1 = (bf16[448,128]{1,0:T(8,128)(2,1)}, bf16[448,512]{1,0:T(8,128)(2,1)}, f32[14,8,512]{2,1,0:T(8,128)}, f32[14,8,512]{2,1,0:T(8,128)}, f32[14,8,512]{2,1...) custom-call(bf16[448,128]{1,0:T(8,128)(2,1)} %get-tuple-element.11.val_ref, ...), custom_call_target="tpu_custom_call" | custom-call | tf_op jit(solution)/shard_map/finish/pallas_call | solution.py:478
  (2 shorter events, 0.0 us)
Async XLA Ops:
  2.3 0.6 copy-start

commit v3 on v2

--- a/solution.py
+++ b/solution.py
@@ -13,8 +13,10 @@
 beta_second = 0.999
 adam_eps = 1e-08
 adam_step = 20.0
-small_lag = 1
-sum_lag = 4
+begin_at = 1
+middle_at = 3
+end_at = 5
+sum_lag = 0
 ln2 = 0.6931471805599453
 inv_ln2 = 1.4426950408889634
 code_bits = 14.0
@@ -83,7 +85,10 @@
     slot_a,
     slot_g,
     ag,
-    sm,
+    sm_part,
+    sm_in,
+    sm_own,
+    sm_all,
     part,
     sum_out,
     sum_in,
@@ -95,10 +100,12 @@
     sem_gr,
     ag_s,
     ag_r,
-    sm_s,
-    sm_r,
     rs_s,
     rs_r,
+    sm_ps,
+    sm_pr,
+    sm_ts,
+    sm_tr,
 ):
     my_dp = lax.axis_index("dp")
     me = lax.axis_index("tensor")
@@ -117,14 +124,17 @@
     load_w.start()
 
     barrier = pltpu.get_barrier_semaphore()
-    pl.semaphore_signal(barrier, inc=1, device_id={"tensor": right}, device_id_type=MESH)
-    pl.semaphore_signal(barrier, inc=1, device_id={"tensor": left}, device_id_type=MESH)
-
     def greet(i, carry):
         other = lax.rem(my_dp + i, n_dp)
         pl.semaphore_signal(barrier, inc=1, device_id={"dp": other}, device_id_type=MESH)
         return carry
 
+    def greet_z(i, carry):
+        other = lax.rem(me + i, n_z)
+        pl.semaphore_signal(barrier, inc=1, device_id={"tensor": other}, device_id_type=MESH)
+        return carry
+
+    lax.fori_loop(1, n_z, greet_z, 0)
     lax.fori_loop(1, n_dp, greet, 0)
 
     at_row = lax.broadcasted_iota(jnp.int32, (block, cols), 0)
@@ -141,7 +151,7 @@
         return carry
 
     lax.fori_loop(0, n_dp, pack, 0)
-    pl.semaphore_wait(barrier, n_dp + 1)
+    pl.semaphore_wait(barrier, n_dp + n_z - 2)
 
     def adapter_copy(other, slot):
         return pltpu.make_async_remote_copy(
@@ -196,8 +206,34 @@
     def gather(step, stream, arriving=False):
         return ring_copy(ag, half, (ag_s, ag_r), stream, step, arriving)
 
-    def small(step, stream, arriving=False):
-        return ring_copy(sm, rank, (sm_s, sm_r), stream, step, arriving)
+    per = sm_own.shape[0]
+
+    def rank_part(other, slot):
+        return pltpu.make_async_remote_copy(
+            src_ref=sm_part.at[other],
+            dst_ref=sm_in.at[slot],
+            send_sem=sm_ps.at[other],
+            recv_sem=sm_pr.at[slot],
+            device_id={"tensor": other},
+            device_id_type=MESH,
+        )
+
+    def rank_sum(other, slot):
+        return pltpu.make_async_remote_copy(
+            src_ref=sm_own,
+            dst_ref=sm_all.at[slot],
+            send_sem=sm_ts.at[other],
+            recv_sem=sm_tr.at[slot],
+            device_id={"tensor": other},
+            device_id_type=MESH,
+        )
+
+    def every_z(action):
+        def body(i, carry):
+            action(lax.rem(me + i, n_z))
+            return carry
+
+        lax.fori_loop(1, n_z, body, 0)
 
     def relay(ring, step):
         for stream in streams:
@@ -277,17 +313,28 @@
             owner = job_ref[my_dp * slots + b] // slots
             slot_a[b * rank : (b + 1) * rank, :] = recv_a[owner].astype(jnp.float32)
         own = slot_a[...].astype(jnp.bfloat16)
-        sm[me, :rank, :] = fold(dot(own[:, :width], tok_ref[...], ((1,), (1,))))
-        sm[me, rank:, :] = fold(dot(own[:, width:], ag[me], ((1,), (1,))))
-        for stream in streams:
-            small(0, stream).start()
+        low = fold(dot(own[:, :width], tok_ref[...], ((1,), (1,))))
+        up = fold(dot(own[:, width:], ag[me], ((1,), (1,))))
+        for r in range(n_z):
+            at = r * per % rank
+            sm_part[r] = (low if r * per < rank else up)[at : at + per]
+        every_z(lambda other: rank_part(other, me).start())
+        sm_in[me] = sm_part[me]
+
+    def small_middle():
+        every_z(lambda other: rank_part(me, other).wait_recv())
+        total = sm_in[0]
+        for c in range(1, n_z):
+            total = total + sm_in[c]
+        sm_own[...] = total
+        every_z(lambda other: rank_sum(other, me).start())
+        sm_all[me] = total
 
     def small_end():
-        total = sm[0]
-        for c in range(1, n_z):
-            total = total + sm[c]
-        low = unfold(total[:rank])
-        up = unfold(total[rank:])
+        every_z(lambda other: rank_sum(me, other).wait_recv())
+        per_half = n_z // 2
+        low = unfold(jnp.concatenate([sm_all[r] for r in range(per_half)], axis=0))
+        up = unfold(jnp.concatenate([sm_all[r] for r in range(per_half, n_z)], axis=0))
         grads = (
             dot_split(up, tok_ref[...], ((1,), (0,))),
             dot_split(low, ag[me], ((1,), (0,))),
@@ -307,10 +354,13 @@
         recv_g[my_dp] = send_g[my_dp]
         return low, up
 
-    def low_rank_terms(low, up):
-        own = slot_a[...].astype(jnp.bfloat16)
-        back[...] += lowrank_scale * dot_split(up, own[:, :width], ((0,), (0,)))
-        part[me] += lowrank_scale * dot_split(low, own[:, width:], ((0,), (0,)))
+    def back_branch(up):
+        own = slot_a[:, :width].astype(jnp.bfloat16)
+        back[...] += lowrank_scale * dot_split(up, own, ((0,), (0,)))
+
+    def value_branch(low):
+        own = slot_a[:, width:].astype(jnp.bfloat16)
+        part[me] += lowrank_scale * dot_split(low, own, ((0,), (0,)))
 
     for stream in streams:
         gather(0, stream).start()
@@ -321,27 +371,27 @@
     forward_for(0)
     backward([0], True)
 
-    for t in range(max(hops + sum_lag, hops + small_lag) + 1):
-        s = t - small_lag
-        if 0 < s <= hops:
-            relay(small, s - 1)
-        if t < hops:
-            relay(gather, t)
+    for t in range(hops + sum_lag + 1):
         u = t - sum_lag
         if 0 <= u <= hops:
             sum_step(u)
-        if s == 0:
+        if t < hops:
+            relay(gather, t)
+        if t == begin_at:
             small_begin()
-        if s == hops:
+        if t == middle_at:
+            small_middle()
+        if t == end_at:
             low, up = small_end()
         if t < hops:
             backward([-1 - t, 1 + t] if t + 1 < hops else [hops])
-        if t < hops:
             forward_for(t + 1)
-        if s == hops:
-            low_rank_terms(low, up)
-
-    tg_ref[...] = back[...].astype(jnp.bfloat16)
+        if t == end_at + 1:
+            back_branch(up)
+        if t == hops - 1:
+            value_branch(low)
+            tg_ref[...] = back[...].astype(jnp.bfloat16)
+
     val_ref[...] = part[me].astype(jnp.bfloat16)
     every_other(lambda other: grad_copy(my_dp, other).wait_recv())
 
@@ -352,10 +402,11 @@
     lax.fori_loop(0, slots, take, 0)
     every_other(lambda other: adapter_copy(other, my_dp).wait_send())
     every_other(lambda other: grad_copy(other, my_dp).wait_send())
+    every_z(lambda other: rank_part(other, me).wait_send())
+    every_z(lambda other: rank_sum(other, me).wait_send())
     for stream in streams:
         for step in range(length(stream)):
             gather(step, stream).wait_send()
-            small(step, stream).wait_send()
             sum_copy(step + hops - length(stream), stream).wait_send()
 
 
@@ -426,6 +477,7 @@
     vmem = pl.BlockSpec(memory_space=pltpu.VMEM)
     whole = pl.BlockSpec(memory_space=pl.ANY)
     hops = n_z // 2
+    per = 2 * rank // n_z
     f32, bf16 = jnp.float32, jnp.bfloat16
     dma = pltpu.SemaphoreType.DMA
     shape = jax.ShapeDtypeStruct
@@ -450,7 +502,10 @@
             pltpu.VMEM((slots * rank, both), f32),
             pltpu.VMEM((slots, rank, both), f32),
             pltpu.VMEM((n_z, rows, cols), bf16),
-            pltpu.VMEM((n_z, 2 * rank, rows), f32),
+            pltpu.VMEM((n_z, per, rows), f32),
+            pltpu.VMEM((n_z, per, rows), f32),
+            pltpu.VMEM((per, rows), f32),
+            pltpu.VMEM((n_z, per, rows), f32),
             pltpu.VMEM((n_z, rows, cols), f32),
             pltpu.VMEM(coded, jnp.int16),
             pltpu.VMEM(coded, jnp.int16),
@@ -458,7 +513,8 @@
             dma((2,)),
         ]
         + [dma((n_dp,))] * 4
-        + [dma((4, hops))] * 6,
+        + [dma((4, hops))] * 4
+        + [dma((n_z,))] * 4,
         compiler_params=pltpu.CompilerParams(collective_id=0, has_side_effects=True),
         name="adapter_step",
     )(

time: 84.5 us -> 71.4 us (0.84)
  Pallas kernels: 81.4 us -> 68.3 us
    pallas_call x1, Pallas kernels: 78.8 us -> 65.7 us  [per_device(): pl.pallas_call(functools.partial(step_kernel, n_dp, n_z), out_shape=(shap...]
where the time goes in v3:
time: 71.4 us; the launch traced here: 71.2 us
  Pallas kernels  68.3 us (96%)
  other arithmetic  2.26 us (3%)
    pallas_call x1, Pallas kernels, per_device(): pl.pallas_call(functools.partial(step_kernel, n_dp, n_z), out_shape=(shap...  65.7 us
    pallas_call x1, Pallas kernels, per_device(): pl.pallas_call(finish_kernel, out_shape=(shape(values.shape, bf16), shape...  2.57 us

profile of v3, /device:TPU:8, one launch (start us, length us, event | category | flops | bytes accessed | tf_op | source)
XLA Modules:
  0.0 71.2 jit_solution(5666640277587926634)
XLA Ops:
  0.6 0.8 %and_select_fusion = s32[14]{0:T(128)S(1)} fusion(s32[448]{0:T(512)} %job_ref.1, s32[]{:T(128)S(6)} %select_n.29), kind=kLoop, calls=%fused_computation.5 | loop fusion | flops 112 | bytes 116 | tf_op jit(solution)/shard_map/jit(floor_divide)/jit(_where)/select_n | solution.py:467
  1.4 0.9 %select_reduce_fusion.group_ref = s32[14]{0:T(128)S(1)} fusion(s32[448]{0:T(512)} %job_ref.1, s32[14]{0:T(128)S(1)} %iota_add_fusion), kind=kLoop, calls=%fused_computation | loop fusion | flops 18802 | bytes 1904 | tf_op jit(solution)/shard_map/reduce_sum | solution.py:471
  2.3 0.0 copy-start
  2.3 0.6 select_reduce_fusion.1
  2.9 0.0 copy-done
  2.9 65.7 %adapter_step.1 = (bf16[448,128]{1,0:T(8,128)(2,1)}, bf16[448,512]{1,0:T(8,128)(2,1)}, f32[14,8,640]{2,1,0:T(8,128)}) custom-call(s32[448]{0:T(512)} %job_ref.1, s32[14]{0:T(128)} %count_ref.1, s32[32]{0:T(128)} %get-tuple-element.15.to_group_ref, s32[32]{0:T(128)} %get-tuple-element.14.to_owner_ref, s32[14]{0:T(128)} %copy-done, bf16[448,512]{1,0:T(8,128)(2,1)} %tok_hbm.1, ...), custom_call_target="tpu_custom_call" | custom-call | tf_op jit(solution)/shard_map/adapter_step/pallas_call | solution.py:486
  68.6 2.6 %finish.1 = (bf16[448,128]{1,0:T(8,128)(2,1)}, bf16[448,512]{1,0:T(8,128)(2,1)}, f32[14,8,512]{2,1,0:T(8,128)}, f32[14,8,512]{2,1,0:T(8,128)}, f32[14,8,512]{2,1...) custom-call(bf16[448,128]{1,0:T(8,128)(2,1)} %get-tuple-element.11.val_ref, ...), custom_call_target="tpu_custom_call" | custom-call | tf_op jit(solution)/shard_map/finish/pallas_call | solution.py:534
  (2 shorter events, 0.0 us)
Async XLA Ops:
  2.3 0.6 copy-start

commit v4 on v3

--- a/solution.py
+++ b/solution.py
@@ -13,9 +13,9 @@
 beta_second = 0.999
 adam_eps = 1e-08
 adam_step = 20.0
-begin_at = 1
-middle_at = 3
-end_at = 5
+begin_at = 2
+middle_at = 4
+end_at = 6
 sum_lag = 0
 ln2 = 0.6931471805599453
 inv_ln2 = 1.4426950408889634

time: 71.4 us -> 74.8 us (1.048)
  the two profiles are of different devices: /device:TPU:8 before, /device:TPU:1 now
where the time goes in v4:
time: 74.8 us; the launch traced here: 74.6 us
  Pallas kernels  71.7 us (96%)
  other arithmetic  2.26 us (3%)
    pallas_call x1, Pallas kernels, per_device(): pl.pallas_call(functools.partial(step_kernel, n_dp, n_z), out_shape=(shap...  69.1 us
    pallas_call x1, Pallas kernels, per_device(): pl.pallas_call(finish_kernel, out_shape=(shape(values.shape, bf16), shape...  2.57 us

profile of v4, /device:TPU:1, one launch (start us, length us, event | category | flops | bytes accessed | tf_op | source)
XLA Modules:
  0.0 74.6 jit_solution(1985968411845904332)
XLA Ops:
  0.6 0.8 %and_select_fusion = s32[14]{0:T(128)S(1)} fusion(s32[448]{0:T(512)} %job_ref.1, s32[]{:T(128)S(6)} %select_n.29), kind=kLoop, calls=%fused_computation.5 | loop fusion | flops 112 | bytes 116 | tf_op jit(solution)/shard_map/jit(floor_divide)/jit(_where)/select_n | solution.py:467
  1.4 0.9 %select_reduce_fusion.group_ref = s32[14]{0:T(128)S(1)} fusion(s32[448]{0:T(512)} %job_ref.1, s32[14]{0:T(128)S(1)} %iota_add_fusion), kind=kLoop, calls=%fused_computation | loop fusion | flops 18802 | bytes 1904 | tf_op jit(solution)/shard_map/reduce_sum | solution.py:471
  2.3 0.0 copy-start
  2.3 0.6 select_reduce_fusion.1
  2.9 0.0 copy-done
  2.9 69.1 %adapter_step.1 = (bf16[448,128]{1,0:T(8,128)(2,1)}, bf16[448,512]{1,0:T(8,128)(2,1)}, f32[14,8,640]{2,1,0:T(8,128)}) custom-call(s32[448]{0:T(512)} %job_ref.1, s32[14]{0:T(128)} %count_ref.1, s32[32]{0:T(128)} %get-tuple-element.15.to_group_ref, s32[32]{0:T(128)} %get-tuple-element.14.to_owner_ref, s32[14]{0:T(128)} %copy-done, bf16[448,512]{1,0:T(8,128)(2,1)} %tok_hbm.1, ...), custom_call_target="tpu_custom_call" | custom-call | tf_op jit(solution)/shard_map/adapter_step/pallas_call | solution.py:486
  72.1 2.6 %finish.1 = (bf16[448,128]{1,0:T(8,128)(2,1)}, bf16[448,512]{1,0:T(8,128)(2,1)}, f32[14,8,512]{2,1,0:T(8,128)}, f32[14,8,512]{2,1,0:T(8,128)}, f32[14,8,512]{2,1...) custom-call(bf16[448,128]{1,0:T(8,128)(2,1)} %get-tuple-element.11.val_ref, ...), custom_call_target="tpu_custom_call" | custom-call | tf_op jit(solution)/shard_map/finish/pallas_call | solution.py:534
  (2 shorter events, 0.0 us)
Async XLA Ops:
  2.3 0.6 copy-start
